TPU v7x, 32 devices: a whole 2x2x4 slice. The times are simulated.
32 devices in a mesh: lat: 8 (over y, x, core), lev: 4 (over z).
Axes of the slice: x: 2, y: 2, z: 4, core: 2. Of those that a mesh axis runs over, the one named last changes fastest.
Arguments:
- tracer: float32 [8, 640, 1280], P('lev', 'lat'), may hold values from -6 to 6
- offsets: int32 [2, 640, 1280], P(None, 'lat'), may hold values from -3 to 3
- stencil: float32 [7, 7], replicated, may hold values from -0.6 to 0.6
- assign: int32 [640], replicated, may hold values from 0 to 639, as said below
- legendre: bfloat16 [640, 2, 320, 320], P('lat', None, 'lev'), may hold values from -0.3125 to 0.3125
- damping: float32 [8], replicated, may hold values from 0.5 to 8
- vert_vecs: float32 [8, 8], replicated, may hold values from -2 to 2
- vert_inv: float32 [8, 8], replicated, may hold values from -2 to 2
Outputs:
- tracer_new: float32 [8, 640, 1280], P('lev', 'lat')
- spectral_new: float32 [640, 2, 320, 16], P('lat', None, 'lev')
Inputs may be any that keep to these rules, and one draw needn't show every extreme that they name: `assign`: a permutation of 0 to 639 in which slots 2 u and 2 u + 1 hold the wavenumbers m and 639 - m.
All inputs are finite; a program needn't handle non-finite values.
Results may differ from a plain program's by a relative error of at most 0.0036.
Values may be sent and summed in bfloat16 or wider, within the bound.
A program may use at most 192 MiB of HBM per device.

v0:
```python
import functools
import math

import jax
import jax.numpy as jnp
from jax import lax
from jax.experimental import pallas as pl
from jax.experimental.pallas import tpu as pltpu
from jax.sharding import PartitionSpec as P

M = 640
LANES = 128
REACH = 3

EXACT = lax.Precision.HIGHEST


def exchange_kernel(axis, count, spread, x_ref, o_ref, send_sems, recv_sems, own_sem):
    me = lax.axis_index(axis)
    barrier = pltpu.get_barrier_semaphore()
    for step in range(1, count):
        peer = lax.rem(me + step, count)
        pl.semaphore_signal(
            barrier, inc=1, device_id={axis: peer}, device_id_type=pl.DeviceIdType.MESH
        )
    pl.semaphore_wait(barrier, count - 1)
    copies = []
    for step in range(1, count):
        peer = lax.rem(me + step, count)
        copy = pltpu.make_async_remote_copy(
            src_ref=x_ref.at[peer] if spread else x_ref,
            dst_ref=o_ref.at[me],
            send_sem=send_sems.at[step - 1],
            recv_sem=recv_sems.at[step - 1],
            device_id={axis: peer},
            device_id_type=pl.DeviceIdType.MESH,
        )
        copy.start()
        copies.append(copy)
    own = pltpu.make_async_copy(x_ref.at[me] if spread else x_ref, o_ref.at[me], own_sem)
    own.start()
    own.wait()
    for copy in copies:
        copy.wait()


def exchange(x, axis, collective_id, spread=True):
    count = lax.axis_size(axis)
    block = x.shape[1:] if spread else x.shape
    return pl.pallas_call(
        functools.partial(exchange_kernel, axis, count, spread),
        out_shape=jax.ShapeDtypeStruct((count,) + block, x.dtype),
        in_specs=[pl.BlockSpec(memory_space=pltpu.VMEM)],
        out_specs=pl.BlockSpec(memory_space=pltpu.VMEM),
        scratch_shapes=[
            pltpu.SemaphoreType.DMA((count - 1,)),
            pltpu.SemaphoreType.DMA((count - 1,)),
            pltpu.SemaphoreType.DMA,
        ],
        compiler_params=pltpu.CompilerParams(
            collective_id=collective_id, has_side_effects=True
        ),
        name="exchange_%d" % collective_id,
    )(x)


def tail_of(wide):
    tail = max(wide - LANES, 0)
    assert tail == 0 or LANES % tail == 0
    return tail


def packed_rows(slots, wide):
    tail = tail_of(wide)
    return 2 * slots + (2 * slots * tail) // LANES


def placement(source, rows, half_lat, band, flip):
    level = jnp.zeros_like(source)
    for k in range(1, 2 + (LANES * 2) // rows):
        level = level + (source >= k * rows).astype(jnp.int32)
    row = source - level * rows
    if flip:
        row = rows - 1 - row
    return level * half_lat + band * rows + row


def one_hot(pick):
    return jnp.where(pick, 1.0, 0.0).astype(jnp.bfloat16)


def split(x):
    high = x.astype(jnp.bfloat16)
    return high, (x - high.astype(jnp.float32)).astype(jnp.bfloat16)


def dot_nt(a, b):
    return lax.dot_general(a, b, (((1,), (1,)), ((), ())), preferred_element_type=jnp.float32)


def dot_nn(a, b):
    return jnp.dot(a, b, preferred_element_type=jnp.float32)


def fill_tables(c1, s1, c2, s2, tables):
    fine_c, fine_s = c2[0], s2[0]
    for a in range(c1.shape[2]):
        lanes = slice(a * LANES, (a + 1) * LANES)
        coarse_c, coarse_s = c1[0, :, a : a + 1], s1[0, :, a : a + 1]
        cosines = coarse_c * fine_c - coarse_s * fine_s
        sines = -(coarse_s * fine_c + coarse_c * fine_s)
        for part, values in enumerate((cosines, sines)):
            high, low = split(values)
            tables[2 * part, :, lanes] = high
            tables[2 * part + 1, :, lanes] = low


def forward_kernel(half, levels, c1, s1, c2, s2, field, o_ref, cells, tables):
    wide = field.shape[0]
    rows = wide // levels
    slots = c1.shape[1]
    padded = cells.shape[1]
    tail = tail_of(wide)
    southern = lax.axis_index("lat") >= half

    @pl.when(pl.program_id(0) == 0)
    def _():
        to = lax.broadcasted_iota(jnp.int32, (padded, wide), 0)
        origin = lax.broadcasted_iota(jnp.int32, (padded, wide), 1)
        level = jnp.zeros_like(to)
        for k in range(1, levels):
            level = level + (to >= k * rows).astype(jnp.int32)
        mirrored = 2 * level * rows + rows - 1 - to
        wanted = jnp.where(southern, mirrored, to)
        pick = one_hot(jnp.logical_and(origin == wanted, to < wide))
        high, low = split(field[...])
        cells[0] = dot_nn(pick, high).astype(jnp.bfloat16)
        cells[1] = dot_nn(pick, low).astype(jnp.bfloat16)

    fill_tables(c1, s1, c2, s2, tables)
    tails = []
    for part in range(2):
        found = (
            dot_nt(tables[2 * part], cells[0])
            + dot_nt(tables[2 * part], cells[1])
            + dot_nt(tables[2 * part + 1], cells[0])
        )
        o_ref[0, part * slots : (part + 1) * slots, :] = found[:, :LANES]
        if tail:
            tails.append(found[:, LANES:])
    if tail:
        groups = LANES // tail
        each = 2 * slots // groups
        both = jnp.concatenate(tails, axis=0)
        total = both[:each]
        for k in range(1, groups):
            total = total + pltpu.roll(both[k * each : (k + 1) * each], k * tail, 1)
        o_ref[0, 2 * slots :, :] = total


def forward(field, levels, trigs, bands, slots):
    wide, cells = field.shape
    padded = LANES * (1 if wide <= LANES else 2)
    rows = packed_rows(slots, wide)
    whole = pl.BlockSpec(field.shape, lambda g: (0, 0))
    per_slot = [pl.BlockSpec((1, slots, t.shape[2]), lambda g: (g, 0, 0)) for t in trigs]
    return pl.pallas_call(
        functools.partial(forward_kernel, bands // 2, levels),
        out_shape=jax.ShapeDtypeStruct((bands, rows, LANES), jnp.float32),
        grid=(bands,),
        in_specs=per_slot + [whole],
        out_specs=pl.BlockSpec((1, rows, LANES), lambda g: (g, 0, 0)),
        scratch_shapes=[
            pltpu.VMEM((2, padded, cells), jnp.bfloat16),
            pltpu.VMEM((4, slots, cells), jnp.bfloat16),
        ],
        name="forward",
    )(*trigs, field)


def hemi_kernel(slots, levels, rows, x_ref, o_ref):
    bands = x_ref.shape[0]
    half = bands // 2
    half_lat = half * rows
    wide = levels * rows
    tail = tail_of(wide)
    length = levels * half_lat
    source = lax.broadcasted_iota(jnp.int32, (LANES, length), 0)
    target = lax.broadcasted_iota(jnp.int32, (LANES, length), 1)
    sums = [None, None]
    for band in range(half):
        north = x_ref[band]
        south = x_ref[bands - 1 - band]
        main = placement(source, rows, half_lat, band, False)
        main = one_hot(jnp.logical_and(target == main, source < wide))
        ends = []
        if tail:
            groups = LANES // tail
            each = 2 * slots // groups
            for k in range(groups):
                cell = source - k * tail + LANES
                lane = placement(cell, rows, half_lat, band, False)
                inside = jnp.logical_and(source >= k * tail, source < (k + 1) * tail)
                ends.append(one_hot(jnp.logical_and(target == lane, inside)))
        for parity, value in enumerate((north + south, north - south)):
            term = dot_nn(value[: 2 * slots].astype(jnp.bfloat16), main)
            if tail:
                end = value[2 * slots :].astype(jnp.bfloat16)
                term = term + jnp.concatenate([dot_nn(end, place) for place in ends], axis=0)
            sums[parity] = term if band == 0 else sums[parity] + term
    for parity in range(2):
        o_ref[parity] = sums[parity].astype(jnp.bfloat16)


def hemispheres(x, slots, levels, rows):
    length = levels * rows * x.shape[0] // 2
    vmem = pl.BlockSpec(memory_space=pltpu.VMEM)
    return pl.pallas_call(
        functools.partial(hemi_kernel, slots, levels, rows),
        out_shape=jax.ShapeDtypeStruct((2, 2 * slots, length), jnp.bfloat16),
        in_specs=[vmem],
        out_specs=vmem,
        name="hemispheres",
    )(x)


def zonal_kernel(slots, levels, rows, x_ref, o_ref):
    planes = x_ref.shape[0]
    bands = o_ref.shape[0]
    half = bands // 2
    half_lat = half * rows
    wide = levels * rows
    tail = tail_of(wide)
    length = levels * half_lat
    totals = []
    for parity in range(2):
        total = x_ref[0, parity].astype(jnp.float32)
        for plane in range(1, planes):
            total = total + x_ref[plane, parity].astype(jnp.float32)
        totals.append(total)
    sides = (totals[0] + totals[1], totals[0] - totals[1])
    source = lax.broadcasted_iota(jnp.int32, (LANES, length), 0)
    target = lax.broadcasted_iota(jnp.int32, (LANES, length), 1)
    for side, value in enumerate(sides):
        flip = side == 1
        groups = LANES // tail if tail else 1
        each = 2 * slots // groups
        whole = value.astype(jnp.bfloat16)
        chunks = [value[k * each : (k + 1) * each].astype(jnp.bfloat16) for k in range(groups)]
        for band in range(half):
            slot = bands - 1 - band if flip else band
            main = placement(source, rows, half_lat, band, flip)
            main = one_hot(jnp.logical_and(target == main, source < wide))
            o_ref[slot, : 2 * slots, :] = dot_nt(whole, main).astype(jnp.bfloat16)
            if tail:
                total = None
                for k in range(groups):
                    cell = source - k * tail + LANES
                    lane = placement(cell, rows, half_lat, band, flip)
                    inside = jnp.logical_and(source >= k * tail, source < (k + 1) * tail)
                    term = dot_nt(chunks[k], one_hot(jnp.logical_and(target == lane, inside)))
                    total = term if k == 0 else total + term
                o_ref[slot, 2 * slots :, :] = total.astype(jnp.bfloat16)


def zonals(x, slots, levels, rows, bands):
    out_rows = packed_rows(slots, levels * rows)
    vmem = pl.BlockSpec(memory_space=pltpu.VMEM)
    return pl.pallas_call(
        functools.partial(zonal_kernel, slots, levels, rows),
        out_shape=jax.ShapeDtypeStruct((bands, out_rows, LANES), jnp.bfloat16),
        in_specs=[vmem],
        out_specs=vmem,
        name="zonals",
    )(x)


def inverse_kernel(c1, s1, c2, s2, x_ref, o_ref, tables):
    wide = o_ref.shape[0]
    slots = c1.shape[1]
    tail = tail_of(wide)
    fill_tables(c1, s1, c2, s2, tables)
    value = x_ref[0].astype(jnp.float32)
    main = value[: 2 * slots]
    pieces = [main]
    if tail:
        groups = LANES // tail
        end = value[2 * slots :]
        spread = [end] + [pltpu.roll(end, LANES - k * tail, 1) for k in range(1, groups)]
        pieces.append(jnp.concatenate(spread, axis=0))
    first = pl.program_id(0) == 0
    for number, piece in enumerate(pieces):
        term = None
        for part in range(2):
            turned = piece[part * slots : (part + 1) * slots].T.astype(jnp.bfloat16)
            for low in range(2):
                one = dot_nn(turned, tables[2 * part + low])
                term = one if term is None else term + one
        begin = number * LANES
        count = min(LANES, wide - begin)
        place = slice(begin, begin + count)

        @pl.when(first)
        def _():
            o_ref[place, :] = term[:count]

        @pl.when(jnp.logical_not(first))
        def _():
            o_ref[place, :] += term[:count]


def inverse(x, trigs, wide, cells):
    bands, rows, _ = x.shape
    slots = trigs[0].shape[1]
    per_slot = [pl.BlockSpec((1, slots, t.shape[2]), lambda g: (g, 0, 0)) for t in trigs]
    return pl.pallas_call(
        inverse_kernel,
        out_shape=jax.ShapeDtypeStruct((wide, cells), jnp.float32),
        grid=(bands,),
        in_specs=per_slot + [pl.BlockSpec((1, rows, LANES), lambda g: (g, 0, 0))],
        out_specs=pl.BlockSpec((wide, cells), lambda g: (0, 0)),
        scratch_shapes=[pltpu.VMEM((4, slots, cells), jnp.bfloat16)],
        name="inverse",
    )(*trigs, x)


def transport_kernel(stencil_ref, band_ref, up_ref, down_ref, code_ref, o_ref, ext, codes, rolled):
    levels, rows, cells = band_ref.shape
    tall = ext.shape[1]
    codes[...] = jnp.full(codes.shape, -1, jnp.int32)
    codes[0:rows, :] = code_ref[...]
    for level in range(levels):
        ext[level, tall - 8 : tall, :] = jnp.zeros((8, cells), jnp.float32)
        ext[level, 0:REACH, :] = up_ref[level]
        ext[level, REACH : REACH + rows, :] = band_ref[level]
        ext[level, REACH + rows : 2 * REACH + rows, :] = down_ref[level]
        for b in range(7):
            whole = ext[level]
            shift = (REACH - b) % cells
            rolled[b, level] = pltpu.roll(whole, shift, 1) if shift else whole

    @pl.loop(0, cells // LANES)
    def _(column):
        lanes = pl.ds(pl.multiple_of(column * LANES, LANES), LANES)
        code = codes[:, lanes]
        sums = [jnp.zeros((tall, LANES), jnp.float32) for _ in range(levels)]
        for a in range(7):
            code_a = pltpu.roll(code, a, 0) if a else code
            terms = [None] * levels
            for b in range(7):
                weight = stencil_ref[a, b]
                factor = jnp.where(code_a == a * 7 + b, weight + 1.0, weight)
                for level in range(levels):
                    term = factor * rolled[b, level, :, lanes]
                    terms[level] = term if b == 0 else terms[level] + term
            for level in range(levels):
                term = pltpu.roll(terms[level], tall - a, 0) if a else terms[level]
                sums[level] = sums[level] + term
        for level in range(levels):
            o_ref[level * rows : (level + 1) * rows, lanes] = sums[level][0:rows]


def transport(band, up, down, offsets, stencil):
    levels, rows, cells = band.shape
    tall = -(-(rows + 2 * REACH) // 8) * 8
    code = (offsets[0] + REACH) * 7 + offsets[1] + REACH
    vmem = pl.BlockSpec(memory_space=pltpu.VMEM)
    return pl.pallas_call(
        transport_kernel,
        out_shape=jax.ShapeDtypeStruct((levels * rows, cells), jnp.float32),
        in_specs=[pl.BlockSpec(memory_space=pltpu.SMEM), vmem, vmem, vmem, vmem],
        out_specs=vmem,
        scratch_shapes=[
            pltpu.VMEM((levels, tall, cells), jnp.float32),
            pltpu.VMEM((tall, cells), jnp.int32),
            pltpu.VMEM((7, levels, tall, cells), jnp.float32),
        ],
        name="transport",
    )(stencil, band, up, down, code)


def halo(cells, width):
    count = lax.axis_size("lat")
    ends = count - 1
    head = cells[:, :width]
    tail = cells[:, cells.shape[1] - width :]
    up = lax.ppermute(tail, "lat", [(i, i + 1) for i in range(ends)])
    down = lax.ppermute(head, "lat", [(i + 1, i) for i in range(ends)])
    return up, down


def trig(steps, assign, lon_cells):
    phase = assign[..., None] * steps % lon_cells
    angles = phase.astype(jnp.float32) * (2.0 * math.pi / lon_cells)
    return jnp.cos(angles), jnp.sin(angles)


def wave_trigs(assign, lon_cells):
    fine = jnp.arange(LANES, dtype=jnp.int32)
    coarse = jnp.arange(lon_cells // LANES, dtype=jnp.int32) * LANES
    c2, s2 = trig(fine, assign, lon_cells)
    c1, s1 = trig(coarse, assign, lon_cells)
    scale = 1.0 / math.sqrt(lon_cells)
    weights = jnp.where(assign == 0, 1.0, 2.0)
    weights = weights.astype(jnp.float32)[..., None]
    c1, s1 = c1 * scale, s1 * scale
    return (c1, s1, c2, s2), (c1 * weights, s1 * weights, c2, s2)


def vertical(spectra, my_waves, first_degree, damping, vert_vecs, vert_inv):
    degree_span = spectra.shape[2]
    degrees = first_degree + jnp.arange(degree_span, dtype=jnp.int32)
    parity = jnp.arange(2, dtype=jnp.int32)
    degree_n = my_waves[:, None, None] + 2 * degrees[None, None, :] + parity[None, :, None]
    inside = (degree_n <= M - 1).astype(jnp.float32)
    forcing = spectra * inside[:, :, :, None, None]
    modal = jnp.einsum("kq,rpicq->rpick", vert_inv, forcing, precision=EXACT)
    scaled_n = degree_n.astype(jnp.float32)
    growth = scaled_n * (scaled_n + 1.0) / float(M * M)
    denominator = 1.0 + growth[:, :, :, None, None] * damping[None, None, None, None, :]
    modal = modal / denominator
    return jnp.einsum("kq,rpicq->rpick", vert_vecs, modal, precision=EXACT)


def on_device(tracer, offsets, stencil, assign, legendre, damping, vert_vecs, vert_inv):
    levels, rows, lon_cells = tracer.shape
    bands = lax.axis_size("lat")
    planes = lax.axis_size("lev")
    slots = legendre.shape[0]
    half = bands // 2
    half_lat = half * rows
    me = lax.axis_index("lat")
    up, down = halo(tracer, REACH)
    to_waves, from_waves = wave_trigs(assign.reshape(bands, slots), lon_cells)
    advected = transport(tracer, up, down, offsets, stencil)
    sent = forward(advected, levels, to_waves, bands, slots)
    got = exchange(sent, "lat", 1)
    hemi = exchange(hemispheres(got, slots, levels, rows), "lev", 2, spread=False)
    hemi = hemi.reshape(planes, 2, 2, slots, levels, half_lat)
    hemi = hemi.transpose(3, 1, 2, 0, 4, 5).reshape(slots, 2, 2, planes * levels, half_lat)

    my_waves = lax.dynamic_slice_in_dim(assign, me * slots, slots)
    first_degree = lax.axis_index("lev") * legendre.shape[2]
    spectra = jnp.einsum(
        "rpij,rpclj->rpicl", legendre, hemi, preferred_element_type=jnp.float32
    )
    solved = vertical(spectra, my_waves, first_degree, damping, vert_vecs, vert_inv)
    packed = solved.astype(jnp.bfloat16)
    back = jnp.einsum(
        "rpij,rpicl->rpclj", legendre, packed, preferred_element_type=jnp.float32
    )
    back = back.astype(jnp.bfloat16).reshape(slots, 2, 2, planes, levels, half_lat)
    back = back.transpose(3, 1, 2, 0, 4, 5).reshape(planes, 2, 2 * slots, levels * half_lat)
    parts = exchange(back, "lev", 3)
    waves = exchange(zonals(parts, slots, levels, rows, bands), "lat", 4)
    tracer_new = inverse(waves, from_waves, levels * rows, lon_cells)
    tracer_new = tracer_new.reshape(levels, rows, lon_cells)
    spectral_new = solved.reshape(slots, 2, solved.shape[2], -1)
    return (tracer_new, spectral_new)


def solution(mesh):
    in_specs = (
        P("lev", "lat", None),
        P(None, "lat", None),
        P(),
        P(),
        P("lat", None, "lev", None),
        P(),
        P(),
        P(),
    )
    out_specs = (P("lev", "lat", None), P("lat", None, "lev", None))
    return jax.shard_map(
        on_device, mesh=mesh, in_specs=in_specs, out_specs=out_specs, check_vma=False
    )
```

profile of v0, /device:TPU:9, one launch (start us, length us, event | category | flops | bytes accessed | tf_op | source)
XLA Modules:
  0.0 193.0 jit_solution(1854725666704034729)
XLA Ops:
  0.7 1.0 fusion.40
  1.7 2.6 %collective-permute-start.1 = (f32[2,3,1280]{2,1,0:T(4,128)S(1)}, f32[2,3,1280]{2,1,0:T(4,128)S(1)}, u32[]{:S(2)}, u32[]{:S(2)}) collective-permute-start(f32[2,3,1280]{2,1,0:T(4,128)S(1)} %get-tuple-element.2), channel_id=1, source_target_pairs={{4,0},{8,4},{12,8},{16,12},{20,16},{24,20},{28,24},{5,1},{9,5},{13... | collective-permute-start | bytes 92168 | tf_op jit(solution)/shard_map/ppermute | solution.py:388
  4.3 3.0 %collective-permute-start = (f32[2,3,1280]{2,1,0:T(4,128)S(1)}, f32[2,3,1280]{2,1,0:T(4,128)S(1)}, u32[]{:S(2)}, u32[]{:S(2)}) collective-permute-start(f32[2,3,1280]{2,1,0:T(4,128)S(1)} %get-tuple-element.3), channel_id=1, source_target_pairs={{0,4},{4,8},{8,12},{12,16},{16,20},{20,24},{24,28},{1,5},{5,9},{9,... | collective-permute-start | bytes 92168 | tf_op jit(solution)/shard_map/ppermute | solution.py:387
  7.3 0.8 mul.131
  8.1 2.3 %fusion.23 = (f32[8,80,128]{2,1,0:T(8,128)}, f32[8,80,128]{2,1,0:T(8,128)}) fusion(s32[8,80]{1,0:T(8,128)S(1)} %mul.131), kind=kLoop, calls=%fused_computation.19 | loop fusion | flops 737280 | bytes 657920 | tf_op jit(solution)/shard_map/sin | solution.py:395
  11.5 0.8 add_bitcast_fusion.code_ref
  12.5 2.1 %fusion.28 = (f32[8,80,10]{2,1,0:T(8,128)}, f32[8,80,10]{2,1,0:T(8,128)}, f32[8,80,10]{2,1,0:T(8,128)}, f32[8,80,10]{2,1,0:T(8,128)}) fusion(f32[8,80,10]{2,1,0:T(8,128)S(1)} %copy.13, f32[8,80]{1,0:T(8,128)S(1)} %select_multiply_fusion), kind=kLoop, calls=%fused_computation.26 | loop fusion | flops 32000 | bytes 130560 | tf_op jit(solution)/shard_map/mul | solution.py:406
  15.9 9.2 %transport.1.field = f32[160,1280]{1,0:T(8,128)} custom-call(f32[7,7]{1,0:T(8,128)} %stencil_ref.1, f32[2,80,1280]{2,1,0:T(8,128)} %band_ref.1, f32[2,3,1280]{2,1,0:T(4,128)} %copy-done.4, f32[2,3,1280]{2,1,0:T(4,128)} %copy-done.3, s32[80,1280]{1,0:T(8,128)} %add_bitcast_fusion.code_ref), custom_call_target="tpu_custom_call" | custom-call | tf_op jit(solution)/shard_map/transport/pallas_call | solution.py:368
  25.1 14.1 %forward.1.x_ref = f32[8,200,128]{2,1,0:T(8,128)} custom-call(f32[8,80,10]{2,1,0:T(8,128)} %get-tuple-element.7.c1, f32[8,80,10]{2,1,0:T(8,128)} %get-tuple-element.6.s1, f32[8,80,128]{2,1,0:T(8,128)} %get-tuple-element.11.c2, f32[8,80,128]{2,1,0:T(8,128)} %get-tuple-element.10.s2, f32[160,1280]{1,0:T(8,128)} %transport.1.field), custom_call_target="tpu_custom_call" | custom-call | tf_op jit(solution)/shard_map/forward/pallas_call | solution.py:167
  39.2 15.2 %exchange_1.1.x_ref = f32[8,200,128]{2,1,0:T(8,128)} custom-call(f32[8,200,128]{2,1,0:T(8,128)} %forward.1.x_ref), custom_call_target="tpu_custom_call" | custom-call | tf_op jit(solution)/shard_map/exchange_1/pallas_call | solution.py:50
  54.4 3.1 %hemispheres.1.x_ref = bf16[2,160,640]{2,1,0:T(8,128)(2,1)} custom-call(f32[8,200,128]{2,1,0:T(8,128)} %exchange_1.1.x_ref), custom_call_target="tpu_custom_call" | custom-call | tf_op jit(solution)/shard_map/hemispheres/pallas_call | solution.py:218
  57.5 40.3 %exchange_2.1 = bf16[4,2,160,640]{3,2,1,0:T(8,128)(2,1)} custom-call(bf16[2,160,640]{2,1,0:T(8,128)(2,1)} %hemispheres.1.x_ref), custom_call_target="tpu_custom_call" | custom-call | tf_op jit(solution)/shard_map/exchange_2/pallas_call | solution.py:50
  97.8 4.4 %reshape.95 = bf16[4,2,2,80,2,320]{5,4,3,2,1,0:T(2,128)(2,1)S(1)} reshape(bf16[4,2,160,640]{3,2,1,0:T(8,128)(2,1)} %exchange_2.1) | data formatting | bytes 3276800 | tf_op jit(solution)/shard_map/reshape | solution.py:439
  102.5 7.2 %fusion.13 = f32[80,2,80,2,8]{2,4,3,1,0:T(8,128)S(1)} fusion(bf16[80,2,80,320]{3,2,1,0:T(8,128)(2,1)} %param.12, bf16[80,2,2,8,320]{4,0,3,2,1:T(8,128)(2,1)S(1)} %bitcast.44, f32[80,2,80]{2,1,0:T(2,128)S(1)} %copy.16), kind=kOutput, calls=%fused_computation.9 | convolution fusion | flops 131276800 | bytes 10700800 | tf_op jit(solution)/shard_map/rpij,rpclj->rpicl/dot_general | solution.py:444
  109.7 1.3 convolution_divide_fusion
  111.0 1.2 fusion.37
  112.2 1.8 fusion.5
  114.1 1.9 reshape.97
  116.0 2.9 %copy.29 = bf16[80,2,2,4,2,320]{5,4,0,2,1,3:T(2,128)(2,1)S(1)} copy(bf16[80,2,2,4,2,320]{5,4,3,2,1,0:T(2,128)(2,1)} %reshape.97) | data formatting | bytes 3276800 | tf_op jit(solution)/shard_map/reshape | solution.py:452
  118.9 2.4 %reshape.98.x_ref = bf16[4,2,160,640]{3,2,1,0:T(8,128)(2,1)} reshape(bf16[4,2,2,80,2,320]{5,4,3,2,1,0:T(2,128)(2,1)S(1)} %bitcast.45) | data formatting | bytes 3276800 | tf_op jit(solution)/shard_map/reshape | solution.py:453
  121.2 41.0 %exchange_3.1.x_ref = bf16[4,2,160,640]{3,2,1,0:T(8,128)(2,1)} custom-call(bf16[4,2,160,640]{3,2,1,0:T(8,128)(2,1)} %reshape.98.x_ref), custom_call_target="tpu_custom_call" | custom-call | tf_op jit(solution)/shard_map/exchange_3/pallas_call | solution.py:50
  162.3 4.1 %zonals.1.x_ref = bf16[8,200,128]{2,1,0:T(8,128)(2,1)} custom-call(bf16[4,2,160,640]{3,2,1,0:T(8,128)(2,1)} %exchange_3.1.x_ref), custom_call_target="tpu_custom_call" | custom-call | tf_op jit(solution)/shard_map/zonals/pallas_call | solution.py:269
  166.4 10.4 %exchange_4.1.x_ref = bf16[8,200,128]{2,1,0:T(8,128)(2,1)} custom-call(bf16[8,200,128]{2,1,0:T(8,128)(2,1)} %zonals.1.x_ref), custom_call_target="tpu_custom_call" | custom-call | tf_op jit(solution)/shard_map/exchange_4/pallas_call | solution.py:50
  176.8 16.2 %inverse.1 = f32[160,1280]{1,0:T(8,128)} custom-call(f32[8,80,10]{2,1,0:T(8,128)} %get-tuple-element.8.c1, f32[8,80,10]{2,1,0:T(8,128)} %get-tuple-element.9.s1, f32[8,80,128]{2,1,0:T(8,128)} %get-tuple-element.11.c2, f32[8,80,128]{2,1,0:T(8,128)} %get-tuple-element.10.s2, bf16[8,200,128]{2,1,0:T(8,128)(2,1)} %exchange_4.1.x_ref), custom_call_target="tpu_custom_call" | custom-call | tf_op jit(solution)/shard_map/inverse/pallas_call | solution.py:316
  (36 shorter events, 2.9 us)
Async XLA Ops:
  0.6 109.0 %copy-start = (f32[8,8]{1,0:T(8,128)S(1)}, f32[8,8]{1,0:T(8,128)}, u32[]{:S(2)}) copy-start(f32[8,8]{1,0:T(8,128)} %param.15) | copy-start | bytes 772
  0.6 10.9 %copy-start.2 = (s32[2,80,1280]{2,1,0:T(8,128)S(1)}, s32[2,80,1280]{2,1,0:T(8,128)}, u32[]{:S(2)}) copy-start(s32[2,80,1280]{2,1,0:T(8,128)} %param.9) | copy-start | bytes 2457604
  0.7 11.7 %copy-start.6 = (f32[8]{0:T(128)S(1)}, f32[8]{0:T(128)}, u32[]{:S(2)}) copy-start(f32[8]{0:T(128)} %param.13) | copy-start | bytes 100
  1.7 13.0 %collective-permute-start.1 = (f32[2,3,1280]{2,1,0:T(4,128)S(1)}, f32[2,3,1280]{2,1,0:T(4,128)S(1)}, u32[]{:S(2)}, u32[]{:S(2)}) collective-permute-start(f32[2,3,1280]{2,1,0:T(4,128)S(1)} %get-tuple-element.2), channel_id=1, source_target_pairs={{4,0},{8,4},{12,8},{16,12},{20,16},{24,20},{28,24},{5,1},{9,5},{13... | collective-permute-start | bytes 92168 | tf_op jit(solution)/shard_map/ppermute | solution.py:388
  4.3 10.4 %collective-permute-start = (f32[2,3,1280]{2,1,0:T(4,128)S(1)}, f32[2,3,1280]{2,1,0:T(4,128)S(1)}, u32[]{:S(2)}, u32[]{:S(2)}) collective-permute-start(f32[2,3,1280]{2,1,0:T(4,128)S(1)} %get-tuple-element.3), channel_id=1, source_target_pairs={{0,4},{4,8},{8,12},{12,16},{16,20},{20,24},{24,28},{1,5},{5,9},{9,... | collective-permute-start | bytes 92168 | tf_op jit(solution)/shard_map/ppermute | solution.py:387
  14.7 0.6 copy-start.3
  15.3 0.6 copy-start.4
  102.2 10.0 %slice-start = ((s8[9830400]{0:T(1024)(128)(4,1)}), s8[4194304]{0:T(1024)(128)(4,1)S(1)}, s32[]{:S(2)}) async-start(s8[9830400]{0:T(1024)(128)(4,1)} %bitcast.41), calls=%async_computation | async-start | bytes 8388608
  102.5 9.7 %slice-start.1 = ((s8[9830400]{0:T(1024)(128)(4,1)}), s8[4194304]{0:T(1024)(128)(4,1)S(1)}, s32[]{:S(2)}) async-start(s8[9830400]{0:T(1024)(128)(4,1)} %bitcast.41), calls=%async_computation.1 | async-start | bytes 8388608
  102.5 9.7 %slice-start.2 = ((s8[9830400]{0:T(1024)(128)(4,1)}), s8[1441792]{0:T(1024)(128)(4,1)S(1)}, s32[]{:S(2)}) async-start(s8[9830400]{0:T(1024)(128)(4,1)} %bitcast.41), calls=%async_computation.2 | async-start | bytes 2883584
  109.7 1.3 copy-start.5
  112.2 1.8 copy-start.1
where the time goes:
time: 194 us; the launch traced here: 193 us
  Pallas kernels  154 us (79%)
  local copies, waits for them, and re-layouts  15.9 us (8%)
  matrix products  11.5 us (6%)
  starting transfers between devices  5.6 us (3%)
  other arithmetic  5.52 us (3%)
    pallas_call x4, Pallas kernels, exchange(): pl.pallas_call(functools.partial(exchange_kernel, axis, count, spread), o...  107 us
    pallas_call x1, Pallas kernels, inverse(): pl.pallas_call(inverse_kernel, out_shape=jax.ShapeDtypeStruct((wide, cell...  16.2 us
    pallas_call x1, Pallas kernels, forward(): pl.pallas_call(functools.partial(forward_kernel, bands // 2, levels), out...  14.1 us
    pallas_call x1, Pallas kernels, transport(): pl.pallas_call(transport_kernel, out_shape=jax.ShapeDtypeStruct((levels *...  9.19 us
    dot_general x1, matrix products, on_device(): jnp.einsum('rpij,rpclj->rpicl', legendre, hemi, preferred_element_type=jn...  7.17 us
    reshape x2, local copies, waits for them, and re-layouts, on_device(): back.astype(jnp.bfloat16).reshape(slots, 2, 2, planes, levels, half_lat)  4.78 us
    reshape x2, local copies, waits for them, and re-layouts, on_device(): hemi = hemi.reshape(planes, 2, 2, slots, levels, half_lat)  4.66 us
    pallas_call x1, Pallas kernels, zonals(): pl.pallas_call(functools.partial(zonal_kernel, slots, levels, rows), out_...  4.15 us
  transfers between devices with their start and end apart: 2, of which 0 were waited for; matrix products, arithmetic and copies ran while one was open for 4% of the time, Pallas kernels for 0%

commit v1 on v0

--- a/solution.py
+++ b/solution.py
@@ -15,7 +15,7 @@
 EXACT = lax.Precision.HIGHEST
 
 
-def exchange_kernel(axis, count, spread, x_ref, o_ref, send_sems, recv_sems, own_sem):
+def exchange_kernel(axis, count, x_ref, o_ref, send_sems, recv_sems, own_sem):
     me = lax.axis_index(axis)
     barrier = pltpu.get_barrier_semaphore()
     for step in range(1, count):
@@ -28,7 +28,7 @@
     for step in range(1, count):
         peer = lax.rem(me + step, count)
         copy = pltpu.make_async_remote_copy(
-            src_ref=x_ref.at[peer] if spread else x_ref,
+            src_ref=x_ref.at[peer],
             dst_ref=o_ref.at[me],
             send_sem=send_sems.at[step - 1],
             recv_sem=recv_sems.at[step - 1],
@@ -37,19 +37,18 @@
         )
         copy.start()
         copies.append(copy)
-    own = pltpu.make_async_copy(x_ref.at[me] if spread else x_ref, o_ref.at[me], own_sem)
+    own = pltpu.make_async_copy(x_ref.at[me], o_ref.at[me], own_sem)
     own.start()
     own.wait()
     for copy in copies:
         copy.wait()
 
 
-def exchange(x, axis, collective_id, spread=True):
+def exchange(x, axis, collective_id):
     count = lax.axis_size(axis)
-    block = x.shape[1:] if spread else x.shape
-    return pl.pallas_call(
-        functools.partial(exchange_kernel, axis, count, spread),
-        out_shape=jax.ShapeDtypeStruct((count,) + block, x.dtype),
+    return pl.pallas_call(
+        functools.partial(exchange_kernel, axis, count),
+        out_shape=jax.ShapeDtypeStruct(x.shape, x.dtype),
         in_specs=[pl.BlockSpec(memory_space=pltpu.VMEM)],
         out_specs=pl.BlockSpec(memory_space=pltpu.VMEM),
         scratch_shapes=[
@@ -64,6 +63,186 @@
     )(x)
 
 
+def greet_neighbours(axis, count, me):
+    barrier = pltpu.get_barrier_semaphore()
+    ways = ((me > 0, me - 1), (me < count - 1, me + 1))
+    for there, peer in ways:
+
+        @pl.when(there)
+        def _():
+            pl.semaphore_signal(
+                barrier, inc=1, device_id={axis: peer}, device_id_type=pl.DeviceIdType.MESH
+            )
+
+    inner = jnp.logical_and(me > 0, me < count - 1)
+
+    @pl.when(inner)
+    def _():
+        pl.semaphore_wait(barrier, 2)
+
+    @pl.when(jnp.logical_not(inner))
+    def _():
+        pl.semaphore_wait(barrier, 1)
+
+
+def gather_kernel(axis, count, x_ref, o_ref, send_sems, recv_sems, own_sem):
+    me = lax.axis_index(axis)
+    greet_neighbours(axis, count, me)
+    own = pltpu.make_async_copy(x_ref, o_ref.at[me], own_sem)
+    own.start()
+
+    def hop(way, k):
+        sign = 1 - 2 * way
+        block, target = me + sign * k, me - sign
+        held = jnp.logical_and(block >= 0, block < count)
+        onward = jnp.logical_and(held, jnp.logical_and(target >= 0, target < count))
+        copy = pltpu.make_async_remote_copy(
+            src_ref=o_ref.at[block] if k else x_ref,
+            dst_ref=o_ref.at[block],
+            send_sem=send_sems.at[way, k],
+            recv_sem=recv_sems.at[way, k],
+            device_id={axis: target},
+            device_id_type=pl.DeviceIdType.MESH,
+        )
+        return held, onward, copy
+
+    def landed(way, k):
+        block = me + (1 - 2 * way) * k
+        return pltpu.make_async_remote_copy(
+            src_ref=x_ref,
+            dst_ref=o_ref.at[block],
+            send_sem=send_sems.at[way, k - 1],
+            recv_sem=recv_sems.at[way, k - 1],
+            device_id={axis: lax.rem(me + 1, count)},
+            device_id_type=pl.DeviceIdType.MESH,
+        )
+
+    for k in range(count):
+        for way in range(2):
+            held, onward, copy = hop(way, k)
+            if k:
+
+                @pl.when(held)
+                def _():
+                    landed(way, k).wait_recv()
+
+            if k < count - 1:
+
+                @pl.when(onward)
+                def _():
+                    copy.start()
+
+    own.wait()
+    for k in range(count - 1):
+        for way in range(2):
+            held, onward, copy = hop(way, k)
+
+            @pl.when(onward)
+            def _():
+                copy.wait_send()
+
+
+def gather(x, axis, collective_id):
+    count = lax.axis_size(axis)
+    return pl.pallas_call(
+        functools.partial(gather_kernel, axis, count),
+        out_shape=jax.ShapeDtypeStruct((count,) + x.shape, x.dtype),
+        in_specs=[pl.BlockSpec(memory_space=pltpu.VMEM)],
+        out_specs=pl.BlockSpec(memory_space=pltpu.VMEM),
+        scratch_shapes=[
+            pltpu.SemaphoreType.DMA((2, count)),
+            pltpu.SemaphoreType.DMA((2, count)),
+            pltpu.SemaphoreType.DMA,
+        ],
+        compiler_params=pltpu.CompilerParams(
+            collective_id=collective_id, has_side_effects=True
+        ),
+        name="gather_%d" % collective_id,
+    )(x)
+
+
+def scatter_kernel(axis, count, x_ref, o_ref, land, outs, send_sems, recv_sems):
+    me = lax.axis_index(axis)
+    greet_neighbours(axis, count, me)
+    fed_from = (me < count - 1, me > 0)
+    parities = x_ref.shape[1]
+
+    def leg(way, dest, source, target):
+        return pltpu.make_async_remote_copy(
+            src_ref=source,
+            dst_ref=land.at[way, dest],
+            send_sem=send_sems.at[way, dest],
+            recv_sem=recv_sems.at[way, dest],
+            device_id={axis: target},
+            device_id_type=pl.DeviceIdType.MESH,
+        )
+
+    legs = []
+    for k in range(count - 1):
+        for way in range(2):
+            dest = k if way == 0 else count - 1 - k
+            away = me > dest if way == 0 else me < dest
+            target = me - 1 if way == 0 else me + 1
+            legs.append((way, dest, away, target))
+
+            @pl.when(jnp.logical_and(away, jnp.logical_not(fed_from[way])))
+            def _():
+                leg(way, dest, x_ref.at[dest], target).start()
+
+            @pl.when(jnp.logical_and(away, fed_from[way]))
+            def _():
+                leg(way, dest, x_ref.at[dest], target).wait_recv()
+
+                @pl.loop(0, parities)
+                def _(parity):
+                    total = land[way, dest, parity].astype(jnp.float32)
+                    total = total + x_ref[dest, parity].astype(jnp.float32)
+                    outs[way, dest, parity] = total.astype(outs.dtype)
+
+                leg(way, dest, outs.at[way, dest], target).start()
+
+    @pl.loop(0, parities)
+    def _(parity):
+        o_ref[parity] = x_ref[me, parity].astype(jnp.float32)
+
+    for way in range(2):
+
+        @pl.when(fed_from[way])
+        def _():
+            leg(way, me, x_ref.at[me], lax.rem(me + 1, count)).wait_recv()
+
+            @pl.loop(0, parities)
+            def _(parity):
+                o_ref[parity] += land[way, me, parity].astype(jnp.float32)
+
+    for way, dest, away, target in legs:
+
+        @pl.when(away)
+        def _():
+            leg(way, dest, outs.at[way, dest], target).wait_send()
+
+
+def scatter(x, axis, collective_id):
+    count = lax.axis_size(axis)
+    vmem = pl.BlockSpec(memory_space=pltpu.VMEM)
+    return pl.pallas_call(
+        functools.partial(scatter_kernel, axis, count),
+        out_shape=jax.ShapeDtypeStruct(x.shape[1:], jnp.float32),
+        in_specs=[vmem],
+        out_specs=vmem,
+        scratch_shapes=[
+            pltpu.VMEM((2,) + x.shape, x.dtype),
+            pltpu.VMEM((2,) + x.shape, x.dtype),
+            pltpu.SemaphoreType.DMA((2, count)),
+            pltpu.SemaphoreType.DMA((2, count)),
+        ],
+        compiler_params=pltpu.CompilerParams(
+            collective_id=collective_id, has_side_effects=True
+        ),
+        name="scatter_%d" % collective_id,
+    )(x)
+
+
 def tail_of(wide):
     tail = max(wide - LANES, 0)
     assert tail == 0 or LANES % tail == 0
@@ -111,11 +290,11 @@
         sines = -(coarse_s * fine_c + coarse_c * fine_s)
         for part, values in enumerate((cosines, sines)):
             high, low = split(values)
-            tables[2 * part, :, lanes] = high
-            tables[2 * part + 1, :, lanes] = low
-
-
-def forward_kernel(half, levels, c1, s1, c2, s2, field, o_ref, cells, tables):
+            tables[0, 2 * part, :, lanes] = high
+            tables[0, 2 * part + 1, :, lanes] = low
+
+
+def forward_kernel(half, levels, c1, s1, c2, s2, field, o_ref, tables, cells):
     wide = field.shape[0]
     rows = wide // levels
     slots = c1.shape[1]
@@ -141,9 +320,9 @@
     tails = []
     for part in range(2):
         found = (
-            dot_nt(tables[2 * part], cells[0])
-            + dot_nt(tables[2 * part], cells[1])
-            + dot_nt(tables[2 * part + 1], cells[0])
+            dot_nt(tables[0, 2 * part], cells[0])
+            + dot_nt(tables[0, 2 * part], cells[1])
+            + dot_nt(tables[0, 2 * part + 1], cells[0])
         )
         o_ref[0, part * slots : (part + 1) * slots, :] = found[:, :LANES]
         if tail:
@@ -166,14 +345,17 @@
     per_slot = [pl.BlockSpec((1, slots, t.shape[2]), lambda g: (g, 0, 0)) for t in trigs]
     return pl.pallas_call(
         functools.partial(forward_kernel, bands // 2, levels),
-        out_shape=jax.ShapeDtypeStruct((bands, rows, LANES), jnp.float32),
+        out_shape=(
+            jax.ShapeDtypeStruct((bands, rows, LANES), jnp.float32),
+            jax.ShapeDtypeStruct((bands, 4, slots, cells), jnp.bfloat16),
+        ),
         grid=(bands,),
         in_specs=per_slot + [whole],
-        out_specs=pl.BlockSpec((1, rows, LANES), lambda g: (g, 0, 0)),
-        scratch_shapes=[
-            pltpu.VMEM((2, padded, cells), jnp.bfloat16),
-            pltpu.VMEM((4, slots, cells), jnp.bfloat16),
-        ],
+        out_specs=(
+            pl.BlockSpec((1, rows, LANES), lambda g: (g, 0, 0)),
+            pl.BlockSpec((1, 4, slots, cells), lambda g: (g, 0, 0, 0)),
+        ),
+        scratch_shapes=[pltpu.VMEM((2, padded, cells), jnp.bfloat16)],
         name="forward",
     )(*trigs, field)
 
@@ -225,20 +407,13 @@
 
 
 def zonal_kernel(slots, levels, rows, x_ref, o_ref):
-    planes = x_ref.shape[0]
     bands = o_ref.shape[0]
     half = bands // 2
     half_lat = half * rows
     wide = levels * rows
     tail = tail_of(wide)
     length = levels * half_lat
-    totals = []
-    for parity in range(2):
-        total = x_ref[0, parity].astype(jnp.float32)
-        for plane in range(1, planes):
-            total = total + x_ref[plane, parity].astype(jnp.float32)
-        totals.append(total)
-    sides = (totals[0] + totals[1], totals[0] - totals[1])
+    sides = (x_ref[0] + x_ref[1], x_ref[0] - x_ref[1])
     source = lax.broadcasted_iota(jnp.int32, (LANES, length), 0)
     target = lax.broadcasted_iota(jnp.int32, (LANES, length), 1)
     for side, value in enumerate(sides):
@@ -275,11 +450,10 @@
     )(x)
 
 
-def inverse_kernel(c1, s1, c2, s2, x_ref, o_ref, tables):
+def inverse_kernel(weights, tables, x_ref, o_ref):
     wide = o_ref.shape[0]
-    slots = c1.shape[1]
+    slots = tables.shape[2]
     tail = tail_of(wide)
-    fill_tables(c1, s1, c2, s2, tables)
     value = x_ref[0].astype(jnp.float32)
     main = value[: 2 * slots]
     pieces = [main]
@@ -292,9 +466,10 @@
     for number, piece in enumerate(pieces):
         term = None
         for part in range(2):
-            turned = piece[part * slots : (part + 1) * slots].T.astype(jnp.bfloat16)
+            weighted = piece[part * slots : (part + 1) * slots] * weights[0]
+            turned = weighted.T.astype(jnp.bfloat16)
             for low in range(2):
-                one = dot_nn(turned, tables[2 * part + low])
+                one = dot_nn(turned, tables[0, 2 * part + low])
                 term = one if term is None else term + one
         begin = number * LANES
         count = min(LANES, wide - begin)
@@ -309,19 +484,21 @@
             o_ref[place, :] += term[:count]
 
 
-def inverse(x, trigs, wide, cells):
+def inverse(x, weights, tables, wide):
     bands, rows, _ = x.shape
-    slots = trigs[0].shape[1]
-    per_slot = [pl.BlockSpec((1, slots, t.shape[2]), lambda g: (g, 0, 0)) for t in trigs]
+    slots, cells = tables.shape[2:]
     return pl.pallas_call(
         inverse_kernel,
         out_shape=jax.ShapeDtypeStruct((wide, cells), jnp.float32),
         grid=(bands,),
-        in_specs=per_slot + [pl.BlockSpec((1, rows, LANES), lambda g: (g, 0, 0))],
+        in_specs=[
+            pl.BlockSpec((1, slots, 1), lambda g: (g, 0, 0)),
+            pl.BlockSpec((1, 4, slots, cells), lambda g: (g, 0, 0, 0)),
+            pl.BlockSpec((1, rows, LANES), lambda g: (g, 0, 0)),
+        ],
         out_specs=pl.BlockSpec((wide, cells), lambda g: (0, 0)),
-        scratch_shapes=[pltpu.VMEM((4, slots, cells), jnp.bfloat16)],
         name="inverse",
-    )(*trigs, x)
+    )(weights, tables, x)
 
 
 def transport_kernel(stencil_ref, band_ref, up_ref, down_ref, code_ref, o_ref, ext, codes, rolled):
@@ -403,8 +580,7 @@
     scale = 1.0 / math.sqrt(lon_cells)
     weights = jnp.where(assign == 0, 1.0, 2.0)
     weights = weights.astype(jnp.float32)[..., None]
-    c1, s1 = c1 * scale, s1 * scale
-    return (c1, s1, c2, s2), (c1 * weights, s1 * weights, c2, s2)
+    return (c1 * scale, s1 * scale, c2, s2), weights
 
 
 def vertical(spectra, my_waves, first_degree, damping, vert_vecs, vert_inv):
@@ -431,11 +607,11 @@
     half_lat = half * rows
     me = lax.axis_index("lat")
     up, down = halo(tracer, REACH)
-    to_waves, from_waves = wave_trigs(assign.reshape(bands, slots), lon_cells)
+    trigs, weights = wave_trigs(assign.reshape(bands, slots), lon_cells)
     advected = transport(tracer, up, down, offsets, stencil)
-    sent = forward(advected, levels, to_waves, bands, slots)
+    sent, tables = forward(advected, levels, trigs, bands, slots)
     got = exchange(sent, "lat", 1)
-    hemi = exchange(hemispheres(got, slots, levels, rows), "lev", 2, spread=False)
+    hemi = gather(hemispheres(got, slots, levels, rows), "lev", 2)
     hemi = hemi.reshape(planes, 2, 2, slots, levels, half_lat)
     hemi = hemi.transpose(3, 1, 2, 0, 4, 5).reshape(slots, 2, 2, planes * levels, half_lat)
 
@@ -451,9 +627,9 @@
     )
     back = back.astype(jnp.bfloat16).reshape(slots, 2, 2, planes, levels, half_lat)
     back = back.transpose(3, 1, 2, 0, 4, 5).reshape(planes, 2, 2 * slots, levels * half_lat)
-    parts = exchange(back, "lev", 3)
-    waves = exchange(zonals(parts, slots, levels, rows, bands), "lat", 4)
-    tracer_new = inverse(waves, from_waves, levels * rows, lon_cells)
+    total = scatter(back, "lev", 3)
+    waves = exchange(zonals(total, slots, levels, rows, bands), "lat", 4)
+    tracer_new = inverse(waves, weights, tables, levels * rows)
     tracer_new = tracer_new.reshape(levels, rows, lon_cells)
     spectral_new = solved.reshape(slots, 2, solved.shape[2], -1)
     return (tracer_new, spectral_new)

time: 194 us -> 189 us (0.974)
  Pallas kernels: 154 us -> 147 us
    pallas_call x4, Pallas kernels: 107 us -> 101 us  [the longest x1 35 us: scatter(): pl.pallas_call(functools.partial(scatter_kernel, axis, count), out_shape=...]
  transfers between devices with their start and end apart: 2 -> 2, of which waited for: 0 -> 0; matrix products, arithmetic and copies ran while one was open for 4% -> 5% of each run, Pallas kernels for 0% -> 0%
where the time goes in v1:
time: 189 us; the launch traced here: 188 us
  Pallas kernels  147 us (78%)
  local copies, waits for them, and re-layouts  16.9 us (9%)
  matrix products  11.3 us (6%)
  other arithmetic  6.47 us (3%)
  starting transfers between devices  5.6 us (3%)
    pallas_call x1, Pallas kernels, scatter(): pl.pallas_call(functools.partial(scatter_kernel, axis, count), out_shape=...  35 us
    pallas_call x2, Pallas kernels, exchange(): pl.pallas_call(functools.partial(exchange_kernel, axis, count), out_shape...  33.5 us
    pallas_call x1, Pallas kernels, gather(): pl.pallas_call(functools.partial(gather_kernel, axis, count), out_shape=j...  32.5 us
    pallas_call x1, Pallas kernels, inverse(): pl.pallas_call(inverse_kernel, out_shape=jax.ShapeDtypeStruct((wide, cell...  15.8 us
    pallas_call x1, Pallas kernels, forward(): pl.pallas_call(functools.partial(forward_kernel, bands // 2, levels), out...  14.1 us
    pallas_call x1, Pallas kernels, transport(): pl.pallas_call(transport_kernel, out_shape=jax.ShapeDtypeStruct((levels *...  9.19 us
    dot_general x1, matrix products, on_device(): jnp.einsum('rpij,rpclj->rpicl', legendre, hemi, preferred_element_type=jn...  7.04 us
    reshape x2, local copies, waits for them, and re-layouts, on_device(): back.astype(jnp.bfloat16).reshape(slots, 2, 2, planes, levels, half_lat)  4.85 us
  transfers between devices with their start and end apart: 2, of which 0 were waited for; matrix products, arithmetic and copies ran while one was open for 5% of the time, Pallas kernels for 0%

profile of v1, /device:TPU:9, one launch (start us, length us, event | category | flops | bytes accessed | tf_op | source)
XLA Modules:
  0.0 188.2 jit_solution(9611235543648924606)
XLA Ops:
  0.6 0.9 fusion.36
  1.6 3.7 %collective-permute-start = (f32[2,3,1280]{2,1,0:T(4,128)S(1)}, f32[2,3,1280]{2,1,0:T(4,128)S(1)}, u32[]{:S(2)}, u32[]{:S(2)}) collective-permute-start(f32[2,3,1280]{2,1,0:T(4,128)S(1)} %get-tuple-element.7), channel_id=1, source_target_pairs={{0,4},{4,8},{8,12},{12,16},{16,20},{20,24},{24,28},{1,5},{5,9},{9,... | collective-permute-start | bytes 92168 | tf_op jit(solution)/shard_map/ppermute | solution.py:564
  5.3 1.9 %collective-permute-start.1 = (f32[2,3,1280]{2,1,0:T(4,128)S(1)}, f32[2,3,1280]{2,1,0:T(4,128)S(1)}, u32[]{:S(2)}, u32[]{:S(2)}) collective-permute-start(f32[2,3,1280]{2,1,0:T(4,128)S(1)} %get-tuple-element.6), channel_id=1, source_target_pairs={{4,0},{8,4},{12,8},{16,12},{20,16},{24,20},{28,24},{5,1},{9,5},{13... | collective-permute-start | bytes 92168 | tf_op jit(solution)/shard_map/ppermute | solution.py:565
  8.9 1.9 %add_bitcast_fusion.code_ref = s32[80,1280]{1,0:T(8,128)} fusion(s32[2,80,1280]{2,1,0:T(8,128)} %param.9), kind=kLoop, calls=%fused_computation.13 | loop fusion | flops 409600 | bytes 1228800 | tf_op jit(solution)/shard_map/add | solution.py:543
  10.8 2.2 %fusion.23 = (f32[8,80,128]{2,1,0:T(8,128)}, f32[8,80,128]{2,1,0:T(8,128)}) fusion(s32[8,80]{1,0:T(8,128)S(1)} %mul.113), kind=kLoop, calls=%fused_computation.19 | loop fusion | flops 737280 | bytes 657920 | tf_op jit(solution)/shard_map/sin | solution.py:572
  13.3 2.0 %sine_multiply_fusion = (f32[8,80,10]{2,1,0:T(8,128)}, f32[8,80,10]{2,1,0:T(8,128)}) fusion(f32[8,80,10]{2,1,0:T(8,128)S(1)} %copy.14), kind=kLoop, calls=%fused_computation.21 | loop fusion | flops 19200 | bytes 76800 | tf_op jit(solution)/shard_map/mul | solution.py:583
  15.6 1.0 select_n.35.weights
  17.8 9.2 %transport.1.field = f32[160,1280]{1,0:T(8,128)} custom-call(f32[7,7]{1,0:T(8,128)} %stencil_ref.1, f32[2,80,1280]{2,1,0:T(8,128)} %band_ref.1, f32[2,3,1280]{2,1,0:T(4,128)} %copy-done.2, f32[2,3,1280]{2,1,0:T(4,128)} %copy-done.3, s32[80,1280]{1,0:T(8,128)} %add_bitcast_fusion.code_ref), custom_call_target="tpu_custom_call" | custom-call | tf_op jit(solution)/shard_map/transport/pallas_call | solution.py:545
  27.0 14.1 %forward.1 = (f32[8,200,128]{2,1,0:T(8,128)}, bf16[8,4,80,1280]{3,2,1,0:T(8,128)(2,1)}) custom-call(f32[8,80,10]{2,1,0:T(8,128)} %get-tuple-element.9.c1, f32[8,80,10]{2,1,0:T(8,128)} %get-tuple-element.8.s1, f32[8,80,128]{2,1,0:T(8,128)} %get-tuple-element.11.c2, f32[8,80,128]{2,1,0:T(8,128)} %get-tuple-element.10.s2, f32[160,1280]{1,0:T(8,128)} %transport.1.field), custom_call_target="tpu_custom_call" | custom-call | tf_op jit(solution)/shard_map/forward/pallas_call | solution.py:346
  41.1 15.8 %exchange_1.1.x_ref = f32[8,200,128]{2,1,0:T(8,128)} custom-call(f32[8,200,128]{2,1,0:T(8,128)} %get-tuple-element.5.x_ref), custom_call_target="tpu_custom_call" | custom-call | tf_op jit(solution)/shard_map/exchange_1/pallas_call | solution.py:49
  56.9 3.1 %hemispheres.1.x_ref = bf16[2,160,640]{2,1,0:T(8,128)(2,1)} custom-call(f32[8,200,128]{2,1,0:T(8,128)} %exchange_1.1.x_ref), custom_call_target="tpu_custom_call" | custom-call | tf_op jit(solution)/shard_map/hemispheres/pallas_call | solution.py:400
  60.0 32.5 %gather_2.1 = bf16[4,2,160,640]{3,2,1,0:T(8,128)(2,1)} custom-call(bf16[2,160,640]{2,1,0:T(8,128)(2,1)} %hemispheres.1.x_ref), custom_call_target="tpu_custom_call" | custom-call | tf_op jit(solution)/shard_map/gather_2/pallas_call | solution.py:147
  92.5 4.4 %reshape.107 = bf16[4,2,2,80,2,320]{5,4,3,2,1,0:T(2,128)(2,1)S(1)} reshape(bf16[4,2,160,640]{3,2,1,0:T(8,128)(2,1)} %gather_2.1) | data formatting | bytes 3276800 | tf_op jit(solution)/shard_map/reshape | solution.py:615
  97.2 7.0 %fusion.13 = f32[80,2,80,2,8]{2,4,3,1,0:T(8,128)S(1)} fusion(bf16[80,2,80,320]{3,2,1,0:T(8,128)(2,1)} %param.12, bf16[80,2,2,8,320]{4,0,3,2,1:T(8,128)(2,1)S(1)} %bitcast.44, f32[80,2,80]{2,1,0:T(2,128)S(1)} %copy.17), kind=kOutput, calls=%fused_computation.9 | convolution fusion | flops 131276800 | bytes 10700800 | tf_op jit(solution)/shard_map/rpij,rpclj->rpicl/dot_general | solution.py:620
  104.3 1.2 convolution_divide_fusion
  105.5 1.2 fusion.33
  106.8 1.8 fusion.5
  108.7 2.0 %reshape.109 = bf16[80,2,2,4,2,320]{5,4,3,2,1,0:T(2,128)(2,1)} reshape(bf16[80,2,2,8,320]{4,3,2,1,0:T(8,128)(2,1)S(1)} %fusion.5) | data formatting | bytes 3276800 | tf_op jit(solution)/shard_map/reshape | solution.py:628
  110.6 2.9 %copy.31 = bf16[80,2,2,4,2,320]{5,4,0,2,1,3:T(2,128)(2,1)S(1)} copy(bf16[80,2,2,4,2,320]{5,4,3,2,1,0:T(2,128)(2,1)} %reshape.109) | data formatting | bytes 3276800 | tf_op jit(solution)/shard_map/reshape | solution.py:628
  113.5 2.4 %reshape.110.x_ref = bf16[4,2,160,640]{3,2,1,0:T(8,128)(2,1)} reshape(bf16[4,2,2,80,2,320]{5,4,3,2,1,0:T(2,128)(2,1)S(1)} %bitcast.45) | data formatting | bytes 3276800 | tf_op jit(solution)/shard_map/reshape | solution.py:629
  115.9 35.0 %scatter_3.1.x_ref = f32[2,160,640]{2,1,0:T(8,128)} custom-call(bf16[4,2,160,640]{3,2,1,0:T(8,128)(2,1)} %reshape.110.x_ref), custom_call_target="tpu_custom_call" | custom-call | tf_op jit(solution)/shard_map/scatter_3/pallas_call | solution.py:228
  150.9 3.8 %zonals.1.x_ref = bf16[8,200,128]{2,1,0:T(8,128)(2,1)} custom-call(f32[2,160,640]{2,1,0:T(8,128)} %scatter_3.1.x_ref), custom_call_target="tpu_custom_call" | custom-call | tf_op jit(solution)/shard_map/zonals/pallas_call | solution.py:444
  154.6 17.8 %exchange_4.1.x_ref = bf16[8,200,128]{2,1,0:T(8,128)(2,1)} custom-call(bf16[8,200,128]{2,1,0:T(8,128)(2,1)} %zonals.1.x_ref), custom_call_target="tpu_custom_call" | custom-call | tf_op jit(solution)/shard_map/exchange_4/pallas_call | solution.py:49
  172.4 15.8 %inverse.1 = f32[160,1280]{1,0:T(8,128)} custom-call(f32[8,80,1]{2,1,0:T(8,128)} %select_n.35.weights, bf16[8,4,80,1280]{3,2,1,0:T(8,128)(2,1)} %get-tuple-element.4.tables, bf16[8,200,128]{2,1,0:T(8,128)(2,1)} %exchange_4.1.x_ref), custom_call_target="tpu_custom_call" | custom-call | tf_op jit(solution)/shard_map/inverse/pallas_call | solution.py:490
  (37 shorter events, 3.6 us)
Async XLA Ops:
  0.6 103.6 %copy-start = (f32[8,8]{1,0:T(8,128)S(1)}, f32[8,8]{1,0:T(8,128)}, u32[]{:S(2)}) copy-start(f32[8,8]{1,0:T(8,128)} %param.15) | copy-start | bytes 772
  1.6 14.9 %collective-permute-start = (f32[2,3,1280]{2,1,0:T(4,128)S(1)}, f32[2,3,1280]{2,1,0:T(4,128)S(1)}, u32[]{:S(2)}, u32[]{:S(2)}) collective-permute-start(f32[2,3,1280]{2,1,0:T(4,128)S(1)} %get-tuple-element.7), channel_id=1, source_target_pairs={{0,4},{4,8},{8,12},{12,16},{16,20},{20,24},{24,28},{1,5},{5,9},{9,... | collective-permute-start | bytes 92168 | tf_op jit(solution)/shard_map/ppermute | solution.py:564
  5.3 11.3 %collective-permute-start.1 = (f32[2,3,1280]{2,1,0:T(4,128)S(1)}, f32[2,3,1280]{2,1,0:T(4,128)S(1)}, u32[]{:S(2)}, u32[]{:S(2)}) collective-permute-start(f32[2,3,1280]{2,1,0:T(4,128)S(1)} %get-tuple-element.6), channel_id=1, source_target_pairs={{4,0},{8,4},{12,8},{16,12},{20,16},{24,20},{28,24},{5,1},{9,5},{13... | collective-permute-start | bytes 92168 | tf_op jit(solution)/shard_map/ppermute | solution.py:565
  8.9 6.5 %copy-start.6 = (f32[8]{0:T(128)S(1)}, f32[8]{0:T(128)}, u32[]{:S(2)}) copy-start(f32[8]{0:T(128)} %param.13) | copy-start | bytes 100
  10.8 4.7 %copy-start.4 = (s32[640]{0:T(1024)S(1)}, s32[640]{0:T(1024)}, u32[]{:S(2)}) copy-start(s32[640]{0:T(1024)} %param.11) | copy-start | bytes 7684
  16.5 0.6 copy-start.2
  17.1 0.6 copy-start.3
  96.9 9.9 %slice-start = ((s8[9830400]{0:T(1024)(128)(4,1)}), s8[4194304]{0:T(1024)(128)(4,1)S(1)}, s32[]{:S(2)}) async-start(s8[9830400]{0:T(1024)(128)(4,1)} %bitcast.41), calls=%async_computation | async-start | bytes 8388608
  97.2 9.6 %slice-start.1 = ((s8[9830400]{0:T(1024)(128)(4,1)}), s8[4194304]{0:T(1024)(128)(4,1)S(1)}, s32[]{:S(2)}) async-start(s8[9830400]{0:T(1024)(128)(4,1)} %bitcast.41), calls=%async_computation.1 | async-start | bytes 8388608
  97.2 9.6 %slice-start.2 = ((s8[9830400]{0:T(1024)(128)(4,1)}), s8[1441792]{0:T(1024)(128)(4,1)S(1)}, s32[]{:S(2)}) async-start(s8[9830400]{0:T(1024)(128)(4,1)} %bitcast.41), calls=%async_computation.2 | async-start | bytes 2883584
  104.3 1.3 copy-start.5
  106.8 1.8 copy-start.1

commit v2 on v1

--- a/solution.py
+++ b/solution.py
@@ -15,7 +15,7 @@
 EXACT = lax.Precision.HIGHEST
 
 
-def exchange_kernel(axis, count, x_ref, o_ref, send_sems, recv_sems, own_sem):
+def exchange_kernel(axis, count, spread, x_ref, o_ref, send_sems, recv_sems, own_sem):
     me = lax.axis_index(axis)
     barrier = pltpu.get_barrier_semaphore()
     for step in range(1, count):
@@ -28,7 +28,7 @@
     for step in range(1, count):
         peer = lax.rem(me + step, count)
         copy = pltpu.make_async_remote_copy(
-            src_ref=x_ref.at[peer],
+            src_ref=x_ref.at[peer] if spread else x_ref,
             dst_ref=o_ref.at[me],
             send_sem=send_sems.at[step - 1],
             recv_sem=recv_sems.at[step - 1],
@@ -37,18 +37,19 @@
         )
         copy.start()
         copies.append(copy)
-    own = pltpu.make_async_copy(x_ref.at[me], o_ref.at[me], own_sem)
+    own = pltpu.make_async_copy(x_ref.at[me] if spread else x_ref, o_ref.at[me], own_sem)
     own.start()
     own.wait()
     for copy in copies:
         copy.wait()
 
 
-def exchange(x, axis, collective_id):
+def exchange(x, axis, collective_id, spread=True):
     count = lax.axis_size(axis)
-    return pl.pallas_call(
-        functools.partial(exchange_kernel, axis, count),
-        out_shape=jax.ShapeDtypeStruct(x.shape, x.dtype),
+    block = x.shape[1:] if spread else x.shape
+    return pl.pallas_call(
+        functools.partial(exchange_kernel, axis, count, spread),
+        out_shape=jax.ShapeDtypeStruct((count,) + block, x.dtype),
         in_specs=[pl.BlockSpec(memory_space=pltpu.VMEM)],
         out_specs=pl.BlockSpec(memory_space=pltpu.VMEM),
         scratch_shapes=[
@@ -83,82 +84,6 @@
     @pl.when(jnp.logical_not(inner))
     def _():
         pl.semaphore_wait(barrier, 1)
-
-
-def gather_kernel(axis, count, x_ref, o_ref, send_sems, recv_sems, own_sem):
-    me = lax.axis_index(axis)
-    greet_neighbours(axis, count, me)
-    own = pltpu.make_async_copy(x_ref, o_ref.at[me], own_sem)
-    own.start()
-
-    def hop(way, k):
-        sign = 1 - 2 * way
-        block, target = me + sign * k, me - sign
-        held = jnp.logical_and(block >= 0, block < count)
-        onward = jnp.logical_and(held, jnp.logical_and(target >= 0, target < count))
-        copy = pltpu.make_async_remote_copy(
-            src_ref=o_ref.at[block] if k else x_ref,
-            dst_ref=o_ref.at[block],
-            send_sem=send_sems.at[way, k],
-            recv_sem=recv_sems.at[way, k],
-            device_id={axis: target},
-            device_id_type=pl.DeviceIdType.MESH,
-        )
-        return held, onward, copy
-
-    def landed(way, k):
-        block = me + (1 - 2 * way) * k
-        return pltpu.make_async_remote_copy(
-            src_ref=x_ref,
-            dst_ref=o_ref.at[block],
-            send_sem=send_sems.at[way, k - 1],
-            recv_sem=recv_sems.at[way, k - 1],
-            device_id={axis: lax.rem(me + 1, count)},
-            device_id_type=pl.DeviceIdType.MESH,
-        )
-
-    for k in range(count):
-        for way in range(2):
-            held, onward, copy = hop(way, k)
-            if k:
-
-                @pl.when(held)
-                def _():
-                    landed(way, k).wait_recv()
-
-            if k < count - 1:
-
-                @pl.when(onward)
-                def _():
-                    copy.start()
-
-    own.wait()
-    for k in range(count - 1):
-        for way in range(2):
-            held, onward, copy = hop(way, k)
-
-            @pl.when(onward)
-            def _():
-                copy.wait_send()
-
-
-def gather(x, axis, collective_id):
-    count = lax.axis_size(axis)
-    return pl.pallas_call(
-        functools.partial(gather_kernel, axis, count),
-        out_shape=jax.ShapeDtypeStruct((count,) + x.shape, x.dtype),
-        in_specs=[pl.BlockSpec(memory_space=pltpu.VMEM)],
-        out_specs=pl.BlockSpec(memory_space=pltpu.VMEM),
-        scratch_shapes=[
-            pltpu.SemaphoreType.DMA((2, count)),
-            pltpu.SemaphoreType.DMA((2, count)),
-            pltpu.SemaphoreType.DMA,
-        ],
-        compiler_params=pltpu.CompilerParams(
-            collective_id=collective_id, has_side_effects=True
-        ),
-        name="gather_%d" % collective_id,
-    )(x)
 
 
 def scatter_kernel(axis, count, x_ref, o_ref, land, outs, send_sems, recv_sems):
@@ -455,33 +380,28 @@
     slots = tables.shape[2]
     tail = tail_of(wide)
     value = x_ref[0].astype(jnp.float32)
-    main = value[: 2 * slots]
-    pieces = [main]
+    both = value[: 2 * slots]
     if tail:
         groups = LANES // tail
         end = value[2 * slots :]
         spread = [end] + [pltpu.roll(end, LANES - k * tail, 1) for k in range(1, groups)]
-        pieces.append(jnp.concatenate(spread, axis=0))
+        both = jnp.concatenate([both, jnp.concatenate(spread, axis=0)], axis=1)
+    term = None
+    for part in range(2):
+        weighted = both[part * slots : (part + 1) * slots] * weights[0]
+        turned = weighted.T[:wide].astype(jnp.bfloat16)
+        for low in range(2):
+            one = dot_nn(turned, tables[0, 2 * part + low])
+            term = one if term is None else term + one
     first = pl.program_id(0) == 0
-    for number, piece in enumerate(pieces):
-        term = None
-        for part in range(2):
-            weighted = piece[part * slots : (part + 1) * slots] * weights[0]
-            turned = weighted.T.astype(jnp.bfloat16)
-            for low in range(2):
-                one = dot_nn(turned, tables[0, 2 * part + low])
-                term = one if term is None else term + one
-        begin = number * LANES
-        count = min(LANES, wide - begin)
-        place = slice(begin, begin + count)
-
-        @pl.when(first)
-        def _():
-            o_ref[place, :] = term[:count]
-
-        @pl.when(jnp.logical_not(first))
-        def _():
-            o_ref[place, :] += term[:count]
+
+    @pl.when(first)
+    def _():
+        o_ref[...] = term
+
+    @pl.when(jnp.logical_not(first))
+    def _():
+        o_ref[...] += term
 
 
 def inverse(x, weights, tables, wide):
@@ -611,7 +531,7 @@
     advected = transport(tracer, up, down, offsets, stencil)
     sent, tables = forward(advected, levels, trigs, bands, slots)
     got = exchange(sent, "lat", 1)
-    hemi = gather(hemispheres(got, slots, levels, rows), "lev", 2)
+    hemi = exchange(hemispheres(got, slots, levels, rows), "lev", 2, spread=False)
     hemi = hemi.reshape(planes, 2, 2, slots, levels, half_lat)
     hemi = hemi.transpose(3, 1, 2, 0, 4, 5).reshape(slots, 2, 2, planes * levels, half_lat)
 

time: 189 us -> 191 us (1.011)
  Pallas kernels: 147 us -> 149 us
    pallas_call x1, Pallas kernels: 15.8 us -> 9.55 us  [inverse(): pl.pallas_call(inverse_kernel, out_shape=jax.ShapeDtypeStruct((wide, cell...]
    pallas_call x1, Pallas kernels: 35 us -> 39.5 us  [scatter(): pl.pallas_call(functools.partial(scatter_kernel, axis, count), out_shape=...]
    pallas_call x3, Pallas kernels: 66.1 us -> 69.5 us  [exchange(): pl.pallas_call(functools.partial(exchange_kernel, axis, count, spread), o...]
where the time goes in v2:
time: 191 us; the launch traced here: 190 us
  Pallas kernels  149 us (78%)
  local copies, waits for them, and re-layouts  16.9 us (9%)
  matrix products  11.5 us (6%)
  other arithmetic  6.47 us (3%)
  starting transfers between devices  5.6 us (3%)
    pallas_call x3, Pallas kernels, exchange(): pl.pallas_call(functools.partial(exchange_kernel, axis, count, spread), o...  69.5 us
    pallas_call x1, Pallas kernels, scatter(): pl.pallas_call(functools.partial(scatter_kernel, axis, count), out_shape=...  39.5 us
    pallas_call x1, Pallas kernels, forward(): pl.pallas_call(functools.partial(forward_kernel, bands // 2, levels), out...  14.1 us
    pallas_call x1, Pallas kernels, inverse(): pl.pallas_call(inverse_kernel, out_shape=jax.ShapeDtypeStruct((wide, cell...  9.55 us
    pallas_call x1, Pallas kernels, transport(): pl.pallas_call(transport_kernel, out_shape=jax.ShapeDtypeStruct((levels *...  9.19 us
    dot_general x1, matrix products, on_device(): jnp.einsum('rpij,rpclj->rpicl', legendre, hemi, preferred_element_type=jn...  7.22 us
    reshape x2, local copies, waits for them, and re-layouts, on_device(): back.astype(jnp.bfloat16).reshape(slots, 2, 2, planes, levels, half_lat)  4.85 us
    reshape x2, local copies, waits for them, and re-layouts, on_device(): hemi = hemi.reshape(planes, 2, 2, slots, levels, half_lat)  4.66 us
  transfers between devices with their start and end apart: 2, of which 0 were waited for; matrix products, arithmetic and copies ran while one was open for 5% of the time, Pallas kernels for 0%

profile of v2, /device:TPU:9, one launch (start us, length us, event | category | flops | bytes accessed | tf_op | source)
XLA Modules:
  0.0 190.1 jit_solution(1700736275734261045)
XLA Ops:
  0.6 0.9 fusion.36
  1.6 3.7 %collective-permute-start = (f32[2,3,1280]{2,1,0:T(4,128)S(1)}, f32[2,3,1280]{2,1,0:T(4,128)S(1)}, u32[]{:S(2)}, u32[]{:S(2)}) collective-permute-start(f32[2,3,1280]{2,1,0:T(4,128)S(1)} %get-tuple-element.7), channel_id=1, source_target_pairs={{0,4},{4,8},{8,12},{12,16},{16,20},{20,24},{24,28},{1,5},{5,9},{9,... | collective-permute-start | bytes 92168 | tf_op jit(solution)/shard_map/ppermute | solution.py:484
  5.3 1.9 %collective-permute-start.1 = (f32[2,3,1280]{2,1,0:T(4,128)S(1)}, f32[2,3,1280]{2,1,0:T(4,128)S(1)}, u32[]{:S(2)}, u32[]{:S(2)}) collective-permute-start(f32[2,3,1280]{2,1,0:T(4,128)S(1)} %get-tuple-element.6), channel_id=1, source_target_pairs={{4,0},{8,4},{12,8},{16,12},{20,16},{24,20},{28,24},{5,1},{9,5},{13... | collective-permute-start | bytes 92168 | tf_op jit(solution)/shard_map/ppermute | solution.py:485
  8.9 1.9 %add_bitcast_fusion.code_ref = s32[80,1280]{1,0:T(8,128)} fusion(s32[2,80,1280]{2,1,0:T(8,128)} %param.9), kind=kLoop, calls=%fused_computation.13 | loop fusion | flops 409600 | bytes 1228800 | tf_op jit(solution)/shard_map/add | solution.py:463
  10.8 2.2 %fusion.23 = (f32[8,80,128]{2,1,0:T(8,128)}, f32[8,80,128]{2,1,0:T(8,128)}) fusion(s32[8,80]{1,0:T(8,128)S(1)} %mul.113), kind=kLoop, calls=%fused_computation.19 | loop fusion | flops 737280 | bytes 657920 | tf_op jit(solution)/shard_map/sin | solution.py:492
  13.3 2.0 %sine_multiply_fusion = (f32[8,80,10]{2,1,0:T(8,128)}, f32[8,80,10]{2,1,0:T(8,128)}) fusion(f32[8,80,10]{2,1,0:T(8,128)S(1)} %copy.14), kind=kLoop, calls=%fused_computation.21 | loop fusion | flops 19200 | bytes 76800 | tf_op jit(solution)/shard_map/mul | solution.py:503
  15.6 1.0 select_n.35.weights
  17.8 9.2 %transport.1.field = f32[160,1280]{1,0:T(8,128)} custom-call(f32[7,7]{1,0:T(8,128)} %stencil_ref.1, f32[2,80,1280]{2,1,0:T(8,128)} %band_ref.1, f32[2,3,1280]{2,1,0:T(4,128)} %copy-done.2, f32[2,3,1280]{2,1,0:T(4,128)} %copy-done.3, s32[80,1280]{1,0:T(8,128)} %add_bitcast_fusion.code_ref), custom_call_target="tpu_custom_call" | custom-call | tf_op jit(solution)/shard_map/transport/pallas_call | solution.py:465
  27.0 14.1 %forward.1 = (f32[8,200,128]{2,1,0:T(8,128)}, bf16[8,4,80,1280]{3,2,1,0:T(8,128)(2,1)}) custom-call(f32[8,80,10]{2,1,0:T(8,128)} %get-tuple-element.9.c1, f32[8,80,10]{2,1,0:T(8,128)} %get-tuple-element.8.s1, f32[8,80,128]{2,1,0:T(8,128)} %get-tuple-element.11.c2, f32[8,80,128]{2,1,0:T(8,128)} %get-tuple-element.10.s2, f32[160,1280]{1,0:T(8,128)} %transport.1.field), custom_call_target="tpu_custom_call" | custom-call | tf_op jit(solution)/shard_map/forward/pallas_call | solution.py:271
  41.1 15.8 %exchange_1.1.x_ref = f32[8,200,128]{2,1,0:T(8,128)} custom-call(f32[8,200,128]{2,1,0:T(8,128)} %get-tuple-element.5.x_ref), custom_call_target="tpu_custom_call" | custom-call | tf_op jit(solution)/shard_map/exchange_1/pallas_call | solution.py:50
  56.9 3.1 %hemispheres.1.x_ref = bf16[2,160,640]{2,1,0:T(8,128)(2,1)} custom-call(f32[8,200,128]{2,1,0:T(8,128)} %exchange_1.1.x_ref), custom_call_target="tpu_custom_call" | custom-call | tf_op jit(solution)/shard_map/hemispheres/pallas_call | solution.py:325
  60.0 40.6 %exchange_2.1 = bf16[4,2,160,640]{3,2,1,0:T(8,128)(2,1)} custom-call(bf16[2,160,640]{2,1,0:T(8,128)(2,1)} %hemispheres.1.x_ref), custom_call_target="tpu_custom_call" | custom-call | tf_op jit(solution)/shard_map/exchange_2/pallas_call | solution.py:50
  100.6 4.4 %reshape.107 = bf16[4,2,2,80,2,320]{5,4,3,2,1,0:T(2,128)(2,1)S(1)} reshape(bf16[4,2,160,640]{3,2,1,0:T(8,128)(2,1)} %exchange_2.1) | data formatting | bytes 3276800 | tf_op jit(solution)/shard_map/reshape | solution.py:535
  105.3 7.2 %fusion.13 = f32[80,2,80,2,8]{2,4,3,1,0:T(8,128)S(1)} fusion(bf16[80,2,80,320]{3,2,1,0:T(8,128)(2,1)} %param.12, bf16[80,2,2,8,320]{4,0,3,2,1:T(8,128)(2,1)S(1)} %bitcast.44, f32[80,2,80]{2,1,0:T(2,128)S(1)} %copy.17), kind=kOutput, calls=%fused_computation.9 | convolution fusion | flops 131276800 | bytes 10700800 | tf_op jit(solution)/shard_map/rpij,rpclj->rpicl/dot_general | solution.py:540
  112.6 1.3 convolution_divide_fusion
  113.8 1.2 fusion.33
  115.1 1.8 fusion.5
  116.9 2.0 %reshape.109 = bf16[80,2,2,4,2,320]{5,4,3,2,1,0:T(2,128)(2,1)} reshape(bf16[80,2,2,8,320]{4,3,2,1,0:T(8,128)(2,1)S(1)} %fusion.5) | data formatting | bytes 3276800 | tf_op jit(solution)/shard_map/reshape | solution.py:548
  118.9 2.9 %copy.31 = bf16[80,2,2,4,2,320]{5,4,0,2,1,3:T(2,128)(2,1)S(1)} copy(bf16[80,2,2,4,2,320]{5,4,3,2,1,0:T(2,128)(2,1)} %reshape.109) | data formatting | bytes 3276800 | tf_op jit(solution)/shard_map/reshape | solution.py:548
  121.8 2.4 %reshape.110.x_ref = bf16[4,2,160,640]{3,2,1,0:T(8,128)(2,1)} reshape(bf16[4,2,2,80,2,320]{5,4,3,2,1,0:T(2,128)(2,1)S(1)} %bitcast.45) | data formatting | bytes 3276800 | tf_op jit(solution)/shard_map/reshape | solution.py:549
  124.2 39.5 %scatter_3.1.x_ref = f32[2,160,640]{2,1,0:T(8,128)} custom-call(bf16[4,2,160,640]{3,2,1,0:T(8,128)(2,1)} %reshape.110.x_ref), custom_call_target="tpu_custom_call" | custom-call | tf_op jit(solution)/shard_map/scatter_3/pallas_call | solution.py:153
  163.6 3.8 %zonals.1.x_ref = bf16[8,200,128]{2,1,0:T(8,128)(2,1)} custom-call(f32[2,160,640]{2,1,0:T(8,128)} %scatter_3.1.x_ref), custom_call_target="tpu_custom_call" | custom-call | tf_op jit(solution)/shard_map/zonals/pallas_call | solution.py:369
  167.4 13.1 %exchange_4.1.x_ref = bf16[8,200,128]{2,1,0:T(8,128)(2,1)} custom-call(bf16[8,200,128]{2,1,0:T(8,128)(2,1)} %zonals.1.x_ref), custom_call_target="tpu_custom_call" | custom-call | tf_op jit(solution)/shard_map/exchange_4/pallas_call | solution.py:50
  180.5 9.6 %inverse.1 = f32[160,1280]{1,0:T(8,128)} custom-call(f32[8,80,1]{2,1,0:T(8,128)} %select_n.35.weights, bf16[8,4,80,1280]{3,2,1,0:T(8,128)(2,1)} %get-tuple-element.4.tables, bf16[8,200,128]{2,1,0:T(8,128)(2,1)} %exchange_4.1.x_ref), custom_call_target="tpu_custom_call" | custom-call | tf_op jit(solution)/shard_map/inverse/pallas_call | solution.py:410
  (37 shorter events, 3.6 us)
Async XLA Ops:
  0.6 111.9 %copy-start = (f32[8,8]{1,0:T(8,128)S(1)}, f32[8,8]{1,0:T(8,128)}, u32[]{:S(2)}) copy-start(f32[8,8]{1,0:T(8,128)} %param.15) | copy-start | bytes 772
  1.6 14.9 %collective-permute-start = (f32[2,3,1280]{2,1,0:T(4,128)S(1)}, f32[2,3,1280]{2,1,0:T(4,128)S(1)}, u32[]{:S(2)}, u32[]{:S(2)}) collective-permute-start(f32[2,3,1280]{2,1,0:T(4,128)S(1)} %get-tuple-element.7), channel_id=1, source_target_pairs={{0,4},{4,8},{8,12},{12,16},{16,20},{20,24},{24,28},{1,5},{5,9},{9,... | collective-permute-start | bytes 92168 | tf_op jit(solution)/shard_map/ppermute | solution.py:484
  5.3 11.3 %collective-permute-start.1 = (f32[2,3,1280]{2,1,0:T(4,128)S(1)}, f32[2,3,1280]{2,1,0:T(4,128)S(1)}, u32[]{:S(2)}, u32[]{:S(2)}) collective-permute-start(f32[2,3,1280]{2,1,0:T(4,128)S(1)} %get-tuple-element.6), channel_id=1, source_target_pairs={{4,0},{8,4},{12,8},{16,12},{20,16},{24,20},{28,24},{5,1},{9,5},{13... | collective-permute-start | bytes 92168 | tf_op jit(solution)/shard_map/ppermute | solution.py:485
  8.9 6.5 %copy-start.6 = (f32[8]{0:T(128)S(1)}, f32[8]{0:T(128)}, u32[]{:S(2)}) copy-start(f32[8]{0:T(128)} %param.13) | copy-start | bytes 100
  10.8 4.7 %copy-start.4 = (s32[640]{0:T(1024)S(1)}, s32[640]{0:T(1024)}, u32[]{:S(2)}) copy-start(s32[640]{0:T(1024)} %param.11) | copy-start | bytes 7684
  16.5 0.6 copy-start.2
  17.1 0.6 copy-start.3
  105.0 10.1 %slice-start = ((s8[9830400]{0:T(1024)(128)(4,1)}), s8[4194304]{0:T(1024)(128)(4,1)S(1)}, s32[]{:S(2)}) async-start(s8[9830400]{0:T(1024)(128)(4,1)} %bitcast.41), calls=%async_computation | async-start | bytes 8388608
  105.3 9.8 %slice-start.1 = ((s8[9830400]{0:T(1024)(128)(4,1)}), s8[4194304]{0:T(1024)(128)(4,1)S(1)}, s32[]{:S(2)}) async-start(s8[9830400]{0:T(1024)(128)(4,1)} %bitcast.41), calls=%async_computation.1 | async-start | bytes 8388608
  105.3 9.8 %slice-start.2 = ((s8[9830400]{0:T(1024)(128)(4,1)}), s8[1441792]{0:T(1024)(128)(4,1)S(1)}, s32[]{:S(2)}) async-start(s8[9830400]{0:T(1024)(128)(4,1)} %bitcast.41), calls=%async_computation.2 | async-start | bytes 2883584
  112.5 1.3 copy-start.5
  115.1 1.8 copy-start.1
